TPU v7x, 256 devices: a whole 4x4x8 slice. The times are simulated.
256 devices in a mesh: code: 32 (over y, z), dp: 8 (over x, core).
Axes of the slice: x: 4, y: 4, z: 8, core: 2. Of those that a mesh axis runs over, the one named last changes fastest.
Arguments:
- codebook: bfloat16 [262144, 768], P(('code', 'dp')), may hold values from -6 to 6
- weight_in: bfloat16 [768, 1024], replicated, may hold values from -0.21875 to 0.21875
- bias_in: float32 [1024], replicated, may hold values from -3 to 3
- weight_out: bfloat16 [1024, 256], replicated, may hold values from -0.1875 to 0.1875
- bias_out: float32 [256], replicated, may hold values from -3 to 3
- latents: float32 [262144, 256], P(('code', 'dp')), may hold values from -6 to 6
- cotangent: float32 [262144, 256], P(('code', 'dp')), may hold values from -6 to 6
- code_owner: int32 [262144, 1], P(('code', 'dp')), may hold values from 0 to 255; in each aligned block of 1024 rows (0 to 1023, 1024 to 2047, ...) at most 8 rows name the same one
- code_row: int32 [262144], P(('code', 'dp')), may hold values from 0 to 1023
Outputs:
- latent_grad: float32 [262144, 256], P(('code', 'dp'))
- grad_weight_in: float32 [768, 1024], replicated
- grad_bias_in: float32 [1024], replicated
- grad_weight_out: float32 [1024, 256], replicated
- grad_bias_out: float32 [256], replicated
Inputs may be any that keep to these rules, and one draw needn't show every extreme that they name: In the rows of one device no owner is named by more than 8 rows, a bound that some block reaches; a latent's code is code_owner * 1024 + code_row.
All inputs are finite; a program needn't handle non-finite values.
Results may differ from a plain program's by a relative error of at most 0.0023.
Values sent between devices are 32-bit elements; how exact they have to be, the bound alone decides.
A program may use at most 128 MiB of HBM per device.

v0:
```python
import jax
import jax.numpy as jnp
from jax import lax
from jax.sharding import PartitionSpec as P

scale_gelu = 0.7978845608028654
cubic_term = 0.044715


def in_blocks(array, dim, size):
    before, after = (array.shape[:dim], array.shape[dim + 1 :])
    return jnp.moveaxis(array.reshape(*before, size, -1, *after), dim, 0)


def in_order(tiles, dim):
    shape = list(tiles.shape[1:])
    shape[dim] *= tiles.shape[0]
    return jnp.moveaxis(tiles, 0, dim).reshape(shape)


def exchange_both(array, axis, axes, splits, concats):
    sizes = [lax.axis_size(a) for a in axes]
    tiles = in_blocks(array, splits[0], sizes[0])
    tiles = jnp.moveaxis(in_blocks(tiles, splits[1] + 1, sizes[1]), 0, 1)
    inside = tiles.shape[2:]
    tiles = tiles.reshape(-1, *inside)
    tiles = lax.all_to_all(tiles, axis, split_axis=0, concat_axis=0, tiled=True)
    tiles = in_order(tiles.reshape(*sizes, *inside), concats[0] + 1)
    return in_order(tiles, concats[1])


def gelu_value(x):
    inner = scale_gelu * (x + cubic_term * x * x * x)
    return 0.5 * x * (1.0 + jnp.tanh(inner))


def gelu_slope(x):
    tangent = jnp.tanh(scale_gelu * (x + cubic_term * x * x * x))
    return 0.5 * (1.0 + tangent) + 0.5 * x * (1.0 - tangent * tangent) * scale_gelu * (
        1.0 + 3.0 * cubic_term * x * x
    )


def per_device(
    codebook, weight_in, bias_in, weight_out, bias_out, latents, cotangent, code_owner, code_row
):
    preact = jnp.dot(codebook, weight_in, preferred_element_type=jnp.float32) + bias_in
    hidden = gelu_value(preact).astype(jnp.bfloat16)
    projected = jnp.dot(hidden, weight_out, preferred_element_type=jnp.float32) + bias_out
    n_code = lax.axis_size("code")
    n_data = lax.axis_size("dp")
    devices = n_code * n_data
    owners = code_owner[:, 0]
    count = owners.shape[0]
    width = latents.shape[1]
    capacity = max(2, 2 * count // devices)
    position = jnp.arange(count, dtype=jnp.int32)
    same = (owners[:, None] == owners[None, :]) & (position[None, :] < position[:, None])
    ranks = jnp.sum(same.astype(jnp.int32), axis=1)
    slots = owners * capacity + ranks
    wanted = jnp.full((devices * capacity,), -1, jnp.int32).at[slots].set(code_row)
    wanted = exchange_both(
        wanted.reshape(n_code, n_data, capacity), ("code", "dp"), ("code", "dp"), (0, 1), (0, 1)
    )
    valid = wanted >= 0
    row_ids = jnp.maximum(wanted, 0).reshape(-1)
    picked = jnp.take(projected, row_ids, axis=0).reshape(n_code, n_data, capacity, width)
    picked = jnp.where(valid[..., None], picked, 0.0)
    answers = exchange_both(picked, ("code", "dp"), ("code", "dp"), (0, 1), (0, 1))
    chosen = jnp.take(answers.reshape(devices * capacity, width), slots, axis=0)
    residual = chosen - latents
    latent_grad = cotangent - 0.25 * residual
    outgoing = (
        jnp.zeros((devices * capacity, width), jnp.float32).at[slots].set(cotangent + residual)
    )
    incoming = exchange_both(
        outgoing.reshape(n_code, n_data, capacity, width),
        ("code", "dp"),
        ("code", "dp"),
        (0, 1),
        (0, 1),
    )
    code_grad = jax.ops.segment_sum(
        incoming.reshape(devices * capacity, width), row_ids, num_segments=projected.shape[0]
    )
    code_low = code_grad.astype(jnp.bfloat16)
    gw_out = lax.dot_general(
        hidden, code_low, (((0,), (0,)), ((), ())), preferred_element_type=jnp.float32
    )
    back = lax.dot_general(
        code_low, weight_out, (((1,), (1,)), ((), ())), preferred_element_type=jnp.float32
    )
    preact_grad = (back * gelu_slope(preact)).astype(jnp.bfloat16)
    gb_in = jnp.sum(preact_grad.astype(jnp.float32), axis=0)
    gw_in = lax.dot_general(
        codebook, preact_grad, (((0,), (0,)), ((), ())), preferred_element_type=jnp.float32
    )
    gb_out = jnp.sum(code_grad, axis=0)
    gw_in, gb_in, gw_out, gb_out = lax.psum((gw_in, gb_in, gw_out, gb_out), ("code", "dp"))
    return (latent_grad, gw_in, gb_in, gw_out, gb_out)


def solution(mesh):
    placed = (
        P(("code", "dp"), None),
        P(),
        P(),
        P(),
        P(),
        P(("code", "dp"), None),
        P(("code", "dp"), None),
        P(("code", "dp"), None),
        P(("code", "dp")),
    )
    return jax.shard_map(
        per_device,
        mesh=mesh,
        in_specs=placed,
        out_specs=(P(("code", "dp"), None), P(), P(), P(), P()),
        check_vma=False,
    )
```

profile of v0, /device:TPU:97, one launch (start us, length us, event | category | flops | bytes accessed | tf_op | source)
XLA Modules:
  0.0 492.3 jit_solution(8340644630260382695)
XLA Ops:
  7.2 1.3 convert_reduce_fusion.1
  8.5 0.7 and_reduce_fusion
  9.2 4.5 scatter_custom_fusion
  13.7 0.8 reshape_transpose_transpose_reshape_reshape_reshape.6
  14.5 14.3 %all-to-all-start = ((s32[256,1,1,8]{3,2,1,0:T(1,128)}), s32[256,1,1,8]{3,2,1,0:T(1,128)S(1)}, u32[]{:S(2)}, u32[]{:S(2)}) async-start(s32[256,1,1,8]{3,2,1,0:T(1,128)} %bitcast.3), calls=%async_computation | async-start | bytes 262144 | tf_op jit(solution)/shard_map/all_to_all | solution.py:27
  28.8 5.9 %multiply_convert_fusion = (bf16[1024,1024]{1,0:T(8,128)(2,1)S(1)}, f32[1024,1024]{1,0:T(8,128)}) fusion(f32[1024]{0:T(1024)} %param.11, bf16[1024,768]{1,0:T(8,128)(2,1)S(1)} %copy-done, bf16[768,1024]{1,0:T(8,128)(2,1)} %param.10), kind=kOutput, calls=%fused_computation.15 | convolution fusion | flops 1621098496 | bytes 9441280 | tf_op jit(solution)/shard_map/dot_general | solution.py:47
  34.7 1.3 copy-done.6
  36.1 0.7 convolution_add_fusion
  36.8 1.8 all-to-all-done
  38.6 0.2 broadcast_compare_fusion
  38.8 0.1 copy.30
  38.9 0.1 broadcast_maximum_fusion
  39.0 0.1 reshape.110
  39.1 0.1 reshape.105
  39.3 0.2 copy.34
  39.5 8.6 %gather_fusion = f32[2048,256]{1,0:T(8,128)} fusion(f32[1024,256]{1,0:T(8,128)S(1)} %convolution_add_fusion, s32[2048]{0:T(1024)S(1)} %broadcast_clamp_fusion), kind=kCustom, calls=%fused_computation | custom fusion | bytes 4202496 | tf_op jit(solution)/shard_map/jit(_take)/gather | solution.py:67
  48.1 4.2 fusion.10
  52.3 12.9 %all-to-all-start.1 = ((f32[256,1,1,8,256]{4,3,2,1,0:T(8,128)}), f32[256,1,1,8,256]{4,3,2,1,0:T(8,128)}, u32[]{:S(2)}, u32[]{:S(2)}) async-start(f32[256,1,1,8,256]{4,3,2,1,0:T(8,128)} %fusion.10), calls=%async_computation.1 | async-start | bytes 4194304 | tf_op jit(solution)/shard_map/all_to_all | solution.py:27
  65.2 49.4 %all-to-all-done.1 = f32[256,1,1,8,256]{4,3,2,1,0:T(8,128)} async-done(((f32[256,1,1,8,256]{4,3,2,1,0:T(8,128)}), f32[256,1,1,8,256]{4,3,2,1,0:T(8,128)}, u32[]{:S(2)}, u32[]{:S(2)}) %all-to-all-start.1) | async-done | bytes 2097184 | tf_op jit(solution)/shard_map/all_to_all | solution.py:27
  114.6 5.1 %gather_fusion.1 = f32[1024,256]{1,0:T(8,128)S(1)} fusion(f32[2048,256]{1,0:T(8,128)} %bitcast.22, s32[1024]{0:T(1024)S(1)} %broadcast_clamp_fusion.1), kind=kCustom, calls=%fused_computation.1 | custom fusion | bytes 2101248 | tf_op jit(solution)/shard_map/jit(_take)/gather | solution.py:70
  119.7 7.5 %scatter_custom_fusion.1 = f32[2048,256]{1,0:T(8,128)} fusion(s32[1024]{0:T(1024)S(1)} %bitcast.77, f32[1024,256]{1,0:T(8,128)} %param.15, f32[]{:T(128)} %constant.32.clone.1, f32[1024,256]{1,0:T(8,128)} %param.14, f32[1024,256]{1,0:T(8,128)S(1)} %gather_fusion.1, f32[]{:T(128)} %constant.31.clone.1, pred[1024]{0:T(1024)(128)(4,1)S(1)} %get-tuple-element.39), kind=kCustom, calls=%fused_computation.25 | custom fusion | flops 786432 | bytes 5243912 | tf_op jit(solution)/shard_map/scatter | solution.py:74
  127.1 60.8 %all_to_all.15 = f32[256,1,1,8,256]{4,3,2,1,0:T(8,128)} all-to-all(f32[256,1,1,8,256]{4,3,2,1,0:T(8,128)} %bitcast.70), channel_id=1, replica_groups=mesh['code'=32,'dp'=8] {'code','dp'}, dimensions={0} | all-to-all | bytes 4194304 | tf_op jit(solution)/shard_map/all_to_all | solution.py:27
  187.9 13.1 %scatter_custom_fusion.2 = f32[1024,256]{1,0:T(8,128)} fusion(s32[2048]{0:T(1024)S(1)} %reshape.110, f32[256,1,1,8,256]{4,3,2,1,0:T(8,128)} %all_to_all.15, f32[]{:T(128)} %constant.32.clone.1), kind=kCustom, calls=%fused_computation.19 | custom fusion | flops 524288 | bytes 3145732 | tf_op jit(solution)/shard_map/scatter-add | solution.py:83
  201.0 3.8 fusion.15
  204.8 3.2 convert_reduce_fusion
  208.0 3.5 convolution_bitcast_fusion
  211.6 2.8 multiply_subtract_fusion
  214.3 1.4 reduce_sum.32
  215.7 74.4 %all-reduce = (f32[1024]{0:T(1024)}, f32[256]{0:T(256)}) all-reduce(f32[1024]{0:T(1024)S(1)} %get-tuple-element.43, f32[256]{0:T(256)S(1)} %reduce_sum.32), channel_id=1, replica_groups=mesh['code'=32,'dp'=8] {'code','dp'}, use_global_device_ids=true, to_apply=%region_6.7 | all-reduce | flops 1280 | bytes 10240 | tf_op jit(solution)/shard_map/psum | solution.py:99
  290.2 190.7 %all-reduce.4.cloned.1.call-done = (f32[768,1024]{0,1:T(8,128)}, f32[1024,256]{1,0:T(8,128)}) async-done(((f32[768,1024]{0,1:T(8,128)}, f32[1024,256]{1,0:T(8,128)}), (f32[768,1024]{0,1:T(8,128)}, f32[1024,256]{1,0:T(8,128)})) %all-reduce.4.cloned.1.call-update) | async-done | bytes 4194320 | tf_op jit(solution)/shard_map/psum | solution.py:99
  480.8 3.6 copy.33
  484.5 1.0 copy.37
  (20 shorter events, 0.1 us)
Async XLA Ops:
  7.2 21.6 %copy-start = (bf16[1024,768]{1,0:T(8,128)(2,1)S(1)}, bf16[1024,768]{1,0:T(8,128)(2,1)}, u32[]{:S(2)}) copy-start(bf16[1024,768]{1,0:T(8,128)(2,1)} %param.9) | copy-start | bytes 4718596
  14.5 24.1 %all-to-all-start = ((s32[256,1,1,8]{3,2,1,0:T(1,128)}), s32[256,1,1,8]{3,2,1,0:T(1,128)S(1)}, u32[]{:S(2)}, u32[]{:S(2)}) async-start(s32[256,1,1,8]{3,2,1,0:T(1,128)} %bitcast.3), calls=%async_computation | async-start | bytes 262144 | tf_op jit(solution)/shard_map/all_to_all | solution.py:27
  28.8 7.3 %copy-start.3 = (bf16[1024,256]{1,0:T(8,128)(2,1)S(1)}, bf16[1024,256]{1,0:T(8,128)(2,1)}, u32[]{:S(2)}) copy-start(bf16[1024,256]{1,0:T(8,128)(2,1)} %param.12) | copy-start | bytes 1572868
  28.8 7.2 %copy-start.5 = (f32[256]{0:T(256)S(1)}, f32[256]{0:T(256)}, u32[]{:S(2)}) copy-start(f32[256]{0:T(256)} %param.13) | copy-start | bytes 3076
  34.7 1.3 copy-start.6
  52.3 62.3 %all-to-all-start.1 = ((f32[256,1,1,8,256]{4,3,2,1,0:T(8,128)}), f32[256,1,1,8,256]{4,3,2,1,0:T(8,128)}, u32[]{:S(2)}, u32[]{:S(2)}) async-start(f32[256,1,1,8,256]{4,3,2,1,0:T(8,128)} %fusion.10), calls=%async_computation.1 | async-start | bytes 4194304 | tf_op jit(solution)/shard_map/all_to_all | solution.py:27
  65.2 415.6 %all-reduce.4.cloned.1.call-start = ((), (), s32[]{:S(2)}) async-start(), calls=%async_computation.3 | async-start | bytes 8388608 | tf_op jit(solution)/shard_map/psum | solution.py:99
  201.0 3.8 copy-start.1
  201.0 3.8 copy-start.4
  201.0 3.8 copy-start.7
  480.8 3.6 copy-start.2
Sparse Core Ops, SparseCore 0:
  211.7 269.0 all-reduce.3
where the time goes:
time: 493 us; the launch traced here: 492 us
  waiting for transfers between devices  242 us (49%)
  blocking collectives  135 us (27%)
  other arithmetic  31.3 us (6%)
  starting transfers between devices  27.2 us (6%)
  local copies, waits for them, and re-layouts  25.3 us (5%)
  matrix products  17.1 us (3%)
  between operations  14.2 us (3%)
    psum x1, waiting for transfers between devices, per_device(): lax.psum((gw_in, gb_in, gw_out, gb_out), ('code', 'dp'))  191 us
    psum x1, blocking collectives, per_device(): lax.psum((gw_in, gb_in, gw_out, gb_out), ('code', 'dp'))  74.4 us
    all_to_all x1, blocking collectives, exchange_both(): tiles = lax.all_to_all(tiles, axis, split_axis=0, concat_axis=0, tiled=True)  60.8 us
    all_to_all x2, waiting for transfers between devices, exchange_both(): tiles = lax.all_to_all(tiles, axis, split_axis=0, concat_axis=0, tiled=True)  51.2 us
    all_to_all x2, starting transfers between devices, exchange_both(): tiles = lax.all_to_all(tiles, axis, split_axis=0, concat_axis=0, tiled=True)  27.2 us
    scatter-add x1, other arithmetic, per_device(): jax.ops.segment_sum(incoming.reshape(devices * capacity, width), row_ids,...  13.1 us
  transfers between devices with their start and end apart: 3, of which 3 were waited for; matrix products, arithmetic and copies ran while one was open for 2% of the time, Pallas kernels for 0%

commit v1 on v0

--- a/solution.py
+++ b/solution.py
@@ -96,7 +96,7 @@
         codebook, preact_grad, (((0,), (0,)), ((), ())), preferred_element_type=jnp.float32
     )
     gb_out = jnp.sum(code_grad, axis=0)
-    gw_in, gb_in, gw_out, gb_out = lax.psum((gw_in, gb_in, gw_out, gb_out), ("code", "dp"))
+    gw_in, gb_in, gw_out, gb_out = lax.psum(lax.psum((gw_in, gb_in, gw_out, gb_out), "code"), "dp")
     return (latent_grad, gw_in, gb_in, gw_out, gb_out)
 
 

time: 493 us -> 478 us (0.970); the launches traced: 492 us -> 468 us
  waiting for transfers between devices: 242 us -> 209 us
  blocking collectives: 135 us -> 144 us
    psum x1 -> x2, waiting for transfers between devices: 191 us -> 158 us  [the longest x1 158 us: per_device(): lax.psum((gw_in, gb_in, gw_out, gb_out), 'code')]
    psum x1 -> x2, blocking collectives: 74.4 us -> 82.9 us  [the longest x1 53.1 us: per_device(): lax.psum((gw_in, gb_in, gw_out, gb_out), 'code')]
  transfers between devices with their start and end apart: 3 -> 4, of which waited for: 3 -> 3; matrix products, arithmetic and copies ran while one was open for 2% -> 2% of each run, Pallas kernels for 0% -> 0%
where the time goes in v1:
time: 478 us; the launch traced here: 468 us
  waiting for transfers between devices  209 us (44%)
  blocking collectives  144 us (30%)
  other arithmetic  31.3 us (7%)
  starting transfers between devices  27.3 us (6%)
  local copies, waits for them, and re-layouts  25.3 us (5%)
  matrix products  17.1 us (4%)
  between operations  14.2 us (3%)
    psum x1, waiting for transfers between devices, per_device(): lax.psum((gw_in, gb_in, gw_out, gb_out), 'code')  158 us
    all_to_all x1, blocking collectives, exchange_both(): tiles = lax.all_to_all(tiles, axis, split_axis=0, concat_axis=0, tiled=True)  60.8 us
    psum x1, blocking collectives, per_device(): lax.psum((gw_in, gb_in, gw_out, gb_out), 'code')  53.1 us
    all_to_all x2, waiting for transfers between devices, exchange_both(): tiles = lax.all_to_all(tiles, axis, split_axis=0, concat_axis=0, tiled=True)  51.2 us
    psum x1, blocking collectives, per_device(): lax.psum(lax.psum((gw_in, gb_in, gw_out, gb_out), 'code'), 'dp')  29.7 us
    all_to_all x2, starting transfers between devices, exchange_both(): tiles = lax.all_to_all(tiles, axis, split_axis=0, concat_axis=0, tiled=True)  27.2 us
    scatter-add x1, other arithmetic, per_device(): jax.ops.segment_sum(incoming.reshape(devices * capacity, width), row_ids,...  13.1 us
  transfers between devices with their start and end apart: 4, of which 3 were waited for; matrix products, arithmetic and copies ran while one was open for 2% of the time, Pallas kernels for 0%

profile of v1, /device:TPU:97, one launch (start us, length us, event | category | flops | bytes accessed | tf_op | source)
XLA Modules:
  0.0 468.1 jit_solution(8280379975380585925)
XLA Ops:
  7.2 1.3 convert_reduce_fusion.1
  8.5 0.7 and_reduce_fusion
  9.2 4.5 scatter_custom_fusion
  13.7 0.8 reshape_transpose_transpose_reshape_reshape_reshape.6
  14.5 14.3 %all-to-all-start = ((s32[256,1,1,8]{3,2,1,0:T(1,128)}), s32[256,1,1,8]{3,2,1,0:T(1,128)S(1)}, u32[]{:S(2)}, u32[]{:S(2)}) async-start(s32[256,1,1,8]{3,2,1,0:T(1,128)} %bitcast.3), calls=%async_computation | async-start | bytes 262144 | tf_op jit(solution)/shard_map/all_to_all | solution.py:27
  28.8 5.9 %multiply_convert_fusion = (bf16[1024,1024]{1,0:T(8,128)(2,1)S(1)}, f32[1024,1024]{1,0:T(8,128)}) fusion(f32[1024]{0:T(1024)} %param.11, bf16[1024,768]{1,0:T(8,128)(2,1)S(1)} %copy-done, bf16[768,1024]{1,0:T(8,128)(2,1)} %param.10), kind=kOutput, calls=%fused_computation.15 | convolution fusion | flops 1621098496 | bytes 9441280 | tf_op jit(solution)/shard_map/dot_general | solution.py:47
  34.7 1.3 copy-done.6
  36.1 0.7 convolution_add_fusion
  36.8 1.8 all-to-all-done
  38.6 0.2 broadcast_compare_fusion
  38.9 0.1 broadcast_maximum_fusion
  39.0 0.1 reshape.110
  39.1 0.1 reshape.105
  39.3 0.2 copy.34
  39.5 8.6 %gather_fusion = f32[2048,256]{1,0:T(8,128)} fusion(f32[1024,256]{1,0:T(8,128)S(1)} %convolution_add_fusion, s32[2048]{0:T(1024)S(1)} %broadcast_clamp_fusion), kind=kCustom, calls=%fused_computation | custom fusion | bytes 4202496 | tf_op jit(solution)/shard_map/jit(_take)/gather | solution.py:67
  48.1 4.2 fusion.10
  52.3 12.9 %all-to-all-start.1 = ((f32[256,1,1,8,256]{4,3,2,1,0:T(8,128)}), f32[256,1,1,8,256]{4,3,2,1,0:T(8,128)}, u32[]{:S(2)}, u32[]{:S(2)}) async-start(f32[256,1,1,8,256]{4,3,2,1,0:T(8,128)} %fusion.10), calls=%async_computation.1 | async-start | bytes 4194304 | tf_op jit(solution)/shard_map/all_to_all | solution.py:27
  65.2 49.4 %all-to-all-done.1 = f32[256,1,1,8,256]{4,3,2,1,0:T(8,128)} async-done(((f32[256,1,1,8,256]{4,3,2,1,0:T(8,128)}), f32[256,1,1,8,256]{4,3,2,1,0:T(8,128)}, u32[]{:S(2)}, u32[]{:S(2)}) %all-to-all-start.1) | async-done | bytes 2097184 | tf_op jit(solution)/shard_map/all_to_all | solution.py:27
  114.6 5.1 %gather_fusion.1 = f32[1024,256]{1,0:T(8,128)S(1)} fusion(f32[2048,256]{1,0:T(8,128)} %bitcast.22, s32[1024]{0:T(1024)S(1)} %broadcast_clamp_fusion.1), kind=kCustom, calls=%fused_computation.1 | custom fusion | bytes 2101248 | tf_op jit(solution)/shard_map/jit(_take)/gather | solution.py:70
  119.7 7.5 %scatter_custom_fusion.1 = f32[2048,256]{1,0:T(8,128)} fusion(s32[1024]{0:T(1024)S(1)} %bitcast.77, f32[1024,256]{1,0:T(8,128)} %param.15, f32[]{:T(128)} %constant.32.clone.1, f32[1024,256]{1,0:T(8,128)} %param.14, f32[1024,256]{1,0:T(8,128)S(1)} %gather_fusion.1, f32[]{:T(128)} %constant.31.clone.1, pred[1024]{0:T(1024)(128)(4,1)S(1)} %get-tuple-element.43), kind=kCustom, calls=%fused_computation.25 | custom fusion | flops 786432 | bytes 5243912 | tf_op jit(solution)/shard_map/scatter | solution.py:74
  127.1 60.8 %all_to_all.15 = f32[256,1,1,8,256]{4,3,2,1,0:T(8,128)} all-to-all(f32[256,1,1,8,256]{4,3,2,1,0:T(8,128)} %bitcast.70), channel_id=1, replica_groups=mesh['code'=32,'dp'=8] {'code','dp'}, dimensions={0} | all-to-all | bytes 4194304 | tf_op jit(solution)/shard_map/all_to_all | solution.py:27
  187.9 13.1 %scatter_custom_fusion.2 = f32[1024,256]{1,0:T(8,128)} fusion(s32[2048]{0:T(1024)S(1)} %reshape.110, f32[256,1,1,8,256]{4,3,2,1,0:T(8,128)} %all_to_all.15, f32[]{:T(128)} %constant.32.clone.1), kind=kCustom, calls=%fused_computation.19 | custom fusion | flops 524288 | bytes 3145732 | tf_op jit(solution)/shard_map/scatter-add | solution.py:83
  201.0 3.7 fusion.15
  204.7 3.2 convert_reduce_fusion
  208.0 3.6 convolution_bitcast_fusion
  211.6 158.1 %all-reduce.7.cloned.1.call-done = (f32[768,1024]{0,1:T(8,128)}, f32[1024,256]{1,0:T(8,128)}) async-done(((f32[768,1024]{0,1:T(8,128)}, f32[1024,256]{1,0:T(8,128)}), (f32[768,1024]{0,1:T(8,128)}, f32[1024,256]{1,0:T(8,128)})) %all-reduce.7.cloned.1.call-update) | async-done | bytes 4194320 | tf_op jit(solution)/shard_map/psum | solution.py:99
  369.7 2.8 multiply_subtract_fusion
  372.4 1.4 reduce_sum.32
  373.8 53.1 %all-reduce = (f32[1024]{0:T(1024)S(1)}, f32[256]{0:T(256)S(1)}) all-reduce(f32[1024]{0:T(1024)S(1)} %get-tuple-element.47, f32[256]{0:T(256)S(1)} %reduce_sum.32), channel_id=1, replica_groups=mesh['code'=32,'dp'=8] {'code'}, use_global_device_ids=true, to_apply=%region_7.8 | all-reduce | flops 1280 | bytes 10240 | tf_op jit(solution)/shard_map/psum | solution.py:99
  427.0 29.7 %all-reduce.2 = (f32[1024]{0:T(1024)}, f32[256]{0:T(256)}) all-reduce(f32[1024]{0:T(1024)S(1)} %get-tuple-element.35, f32[256]{0:T(256)S(1)} %get-tuple-element.36), channel_id=1, replica_groups=mesh['code'=32,'dp'=8] {'dp'}, use_global_device_ids=true, to_apply=%region_8.9 | all-reduce | flops 1280 | bytes 10240 | tf_op jit(solution)/shard_map/psum | solution.py:99
  456.7 3.6 copy.33
  460.3 1.0 copy.39
  (24 shorter events, 0.3 us)
Async XLA Ops:
  7.2 21.6 %copy-start = (bf16[1024,768]{1,0:T(8,128)(2,1)S(1)}, bf16[1024,768]{1,0:T(8,128)(2,1)}, u32[]{:S(2)}) copy-start(bf16[1024,768]{1,0:T(8,128)(2,1)} %param.9) | copy-start | bytes 4718596
  14.5 24.1 %all-to-all-start = ((s32[256,1,1,8]{3,2,1,0:T(1,128)}), s32[256,1,1,8]{3,2,1,0:T(1,128)S(1)}, u32[]{:S(2)}, u32[]{:S(2)}) async-start(s32[256,1,1,8]{3,2,1,0:T(1,128)} %bitcast.3), calls=%async_computation | async-start | bytes 262144 | tf_op jit(solution)/shard_map/all_to_all | solution.py:27
  28.8 7.3 %copy-start.3 = (bf16[1024,256]{1,0:T(8,128)(2,1)S(1)}, bf16[1024,256]{1,0:T(8,128)(2,1)}, u32[]{:S(2)}) copy-start(bf16[1024,256]{1,0:T(8,128)(2,1)} %param.12) | copy-start | bytes 1572868
  28.8 7.2 %copy-start.5 = (f32[256]{0:T(256)S(1)}, f32[256]{0:T(256)}, u32[]{:S(2)}) copy-start(f32[256]{0:T(256)} %param.13) | copy-start | bytes 3076
  34.7 1.3 copy-start.6
  52.3 62.3 %all-to-all-start.1 = ((f32[256,1,1,8,256]{4,3,2,1,0:T(8,128)}), f32[256,1,1,8,256]{4,3,2,1,0:T(8,128)}, u32[]{:S(2)}, u32[]{:S(2)}) async-start(f32[256,1,1,8,256]{4,3,2,1,0:T(8,128)} %fusion.10), calls=%async_computation.1 | async-start | bytes 4194304 | tf_op jit(solution)/shard_map/all_to_all | solution.py:27
  65.2 304.5 %all-reduce.7.cloned.1.call-start = ((), (), s32[]{:S(2)}) async-start(), calls=%async_computation.3 | async-start | bytes 8388608 | tf_op jit(solution)/shard_map/psum | solution.py:99
  201.0 3.7 copy-start.1
  201.0 3.7 copy-start.4
  201.0 3.7 copy-start.7
  211.6 245.1 %all-reduce.9.cloned.1.call-start = ((), (), s32[]{:S(2)}) async-start(), calls=%async_computation.4 | async-start | bytes 8388608 | tf_op jit(solution)/shard_map/psum | solution.py:99
  456.7 3.6 copy-start.2
Sparse Core Ops, SparseCore 0:
  211.7 157.9 all-reduce.6
  372.1 76.5 all-reduce.8
